TPU v7x, 32 devices: a whole 2x2x4 slice. The times are simulated.
32 devices in a mesh: row: 8 (over z, y), col: 4 (over x, core).
Axes of the slice: x: 2, y: 2, z: 4, core: 2. Of those that a mesh axis runs over, the one named last changes fastest.
Arguments:
- pair_rep: bfloat16 [1024, 1024, 128], P('row', 'col'), may hold values from -8 to 8
- row_ids: int32 [16], P('row'), may hold values from 0 to 1023, as said below
- pad_mask: int32 [1024], P('col'), may hold values from 0 to 1, as said below
- ln_gain: float32 [128], replicated, may hold values from 0.25 to 1.75
- ln_bias: float32 [128], replicated, may hold values from -2 to 2
- w_query: bfloat16 [128, 128], replicated, may hold values from -2 to 2
- w_key: bfloat16 [128, 128], replicated, may hold values from -2 to 2
- w_value: bfloat16 [128, 128], replicated, may hold values from -0.5 to 0.5
- w_gate: bfloat16 [128, 128], replicated, may hold values from -0.5 to 0.5
- gate_bias: float32 [128], replicated, may hold values from -4 to 4
- w_bias: bfloat16 [128, 4], replicated, may hold values from -0.5 to 0.5
- w_out: bfloat16 [128, 128], replicated, may hold values from -0.5 to 0.5
Outputs:
- update: bfloat16 [16, 1024, 128], P('col', 'row')
Inputs may be any that keep to these rules, and one draw needn't show every extreme that they name: `row_ids`: entries t * 2 to t * 2 + 1 are distinct and lie in [t * 128, (t + 1) * 128). `pad_mask`: A prefix of the tokens is real and the rest is padding; the first 257 tokens are real.
All inputs are finite; a program needn't handle non-finite values.
Results may differ from a plain program's by a relative error of at most 0.023.
Values may be sent and summed in bfloat16 or wider, within the bound.
A program may use at most 128 MiB of HBM per device.

v0:
```python
import jax
import jax.numpy as jnp
from jax import lax
from jax.sharding import PartitionSpec as P


def from_root(value, axis, source):
    kept = jnp.where(lax.axis_index(axis) == source, value, 0).astype(value.dtype)
    return lax.psum(kept, axis)


def merged(value, axis, join):
    gathered = jax.tree.map(
        lambda a, kind: lax.all_gather(a.astype(kind), axis),
        value,
        (jnp.bfloat16, jnp.bfloat16, jnp.bfloat16),
    )

    def take(source):
        return jax.tree.map(
            lambda a, own: lax.dynamic_index_in_dim(a, source, 0, False).astype(own.dtype),
            gathered,
            value,
        )

    return lax.fori_loop(
        1, lax.axis_size(axis), lambda source, state: join(state, take(source)), take(0)
    )


def layer_norm(values, ln_gain, ln_bias):
    values = values.astype(jnp.float32)
    centre = jnp.mean(values, axis=-1, keepdims=True)
    spread = jnp.mean((values - centre) ** 2, axis=-1, keepdims=True)
    return ((values - centre) * lax.rsqrt(spread + 1e-05) * ln_gain + ln_bias).astype(jnp.bfloat16)


def project(normed, weight):
    flat = normed.reshape(-1, normed.shape[-1])
    return jnp.dot(flat, weight, preferred_element_type=jnp.float32).reshape(
        normed.shape[:-1] + (weight.shape[1],)
    )


def query_gate(normed, w_query, w_gate, gate_bias, head_dim):
    query = (project(normed, w_query) / jnp.sqrt(jnp.float32(head_dim))).astype(jnp.bfloat16)
    gate = jax.nn.sigmoid(project(normed, w_gate) + gate_bias).astype(jnp.bfloat16)
    return jnp.concatenate([query, gate], axis=-1)


def key_value(normed, w_key, w_value):
    return jnp.concatenate(
        [
            project(normed, w_key).astype(jnp.bfloat16),
            project(normed, w_value).astype(jnp.bfloat16),
        ],
        axis=-1,
    )


def combine_parts(first, second):
    peak_a, total_a, summed_a = first
    peak_b, total_b, summed_b = second
    peak = jnp.maximum(peak_a, peak_b)
    scale_a = jnp.exp(peak_a - peak)
    scale_b = jnp.exp(peak_b - peak)
    return (
        peak,
        total_a * scale_a + total_b * scale_b,
        summed_a * scale_a[..., None] + summed_b * scale_b[..., None],
    )


def body(
    pair_rep,
    row_ids,
    pad_mask,
    ln_gain,
    ln_bias,
    w_query,
    w_key,
    w_value,
    w_gate,
    gate_bias,
    w_bias,
    w_out,
):
    rows_here = pair_rep.shape[0]
    cols_here = pair_rep.shape[1]
    heads = w_bias.shape[1]
    width = w_query.shape[1]
    head_dim = width // heads
    n_col = lax.axis_size("col")
    row_index = lax.axis_index("row")
    col_index = lax.axis_index("col")
    normed = layer_norm(pair_rep, ln_gain, ln_bias)
    offsets = row_ids - row_index * rows_here
    slice_start = row_index * rows_here % cols_here
    root_col = row_index * rows_here // cols_here
    raw_chosen = jnp.take(pair_rep, offsets, axis=0)
    raw_all = lax.all_gather(raw_chosen, "row", axis=0, tiled=True)
    keys_values = key_value(layer_norm(raw_all, ln_gain, ln_bias), w_key, w_value)
    raw_mine = lax.dynamic_slice_in_dim(raw_all, slice_start, rows_here, 1)
    raw_mine = from_root(raw_mine, "col", root_col)
    query_gates = query_gate(
        layer_norm(raw_mine, ln_gain, ln_bias), w_query, w_gate, gate_bias, head_dim
    )
    selected = query_gates.shape[0]
    pair_bias = jnp.einsum("jkc,ch->hjk", normed, w_bias, preferred_element_type=jnp.float32)
    key_live = pad_mask > 0
    query = query_gates[..., :width].reshape(4, selected // 4, rows_here, heads, head_dim)
    gate = query_gates[..., width:]
    key_rows = keys_values[..., :width].reshape(4, selected // 4, cols_here, heads, head_dim)
    value_rows = keys_values[..., width:].reshape(4, selected // 4, cols_here, heads, head_dim)

    def partial_block(items):
        query_block, key_block, value_block = items
        scores = jnp.einsum(
            "tjhd,tkhd->thjk", query_block, key_block, preferred_element_type=jnp.float32
        )
        scores = scores + pair_bias[None]
        scores = jnp.where(key_live[None, None, None, :], scores, jnp.float32(-1000000000.0))
        peak = jnp.max(scores, axis=-1)
        expo = jnp.exp(scores - peak[..., None])
        totals = jnp.sum(expo, axis=-1)
        summed = jnp.einsum(
            "thjk,tkhd->thjd",
            expo.astype(jnp.bfloat16),
            value_block,
            preferred_element_type=jnp.float32,
        )
        return (peak, totals, summed)

    peak, totals, summed = lax.map(partial_block, (query, key_rows, value_rows))
    peak = peak.reshape(selected, heads, rows_here)
    totals = totals.reshape(selected, heads, rows_here)
    summed = summed.reshape(selected, heads, rows_here, head_dim)
    row_count = selected // n_col
    peak, totals, summed = merged((peak, totals, summed), "col", combine_parts)
    totals = lax.dynamic_slice_in_dim(totals, col_index * row_count, row_count, 0)
    summed = lax.dynamic_slice_in_dim(summed, col_index * row_count, row_count, 0)
    attended = summed / totals[..., None]
    attended = jnp.transpose(attended, (0, 2, 1, 3)).reshape(row_count, rows_here, width)
    gate_mine = lax.dynamic_slice_in_dim(gate, col_index * row_count, row_count, 0)
    gated = (gate_mine.astype(jnp.float32) * attended).astype(jnp.bfloat16)
    return project(gated, w_out).astype(jnp.bfloat16)


def solution(mesh):
    return jax.shard_map(
        body,
        mesh=mesh,
        in_specs=(
            P("row", "col", None),
            P("row"),
            P("col"),
            P(),
            P(),
            P(),
            P(),
            P(),
            P(),
            P(),
            P(),
            P(),
        ),
        out_specs=P("col", "row", None),
        check_vma=False,
    )
```

profile of v0, /device:TPU:0, one launch (start us, length us, event | category | flops | bytes accessed | tf_op | source)
XLA Modules:
  0.0 170.1 jit_solution(14934871690667444920)
XLA Ops:
  6.5 0.7 compare_and_fusion
  7.2 4.0 %gather_fusion = bf16[2,256,128]{2,1,0:T(8,128)(2,1)S(1)} fusion(bf16[128,256,128]{2,1,0:T(8,128)(2,1)} %param.16, s32[1024]{0:T(1024)S(1)} %pad_clamp_fusion), kind=kCustom, calls=%fused_computation | custom fusion | bytes 262152 | tf_op jit(solution)/shard_map/jit(_take)/gather | solution.py:100
  11.2 0.7 broadcast_select_fusion
  12.0 5.7 %convert_reduce_fusion = f32[128,256]{1,0:T(8,128)S(1)} fusion(bf16[128,256,128]{2,1,0:T(8,128)(2,1)} %param.16), kind=kLoop, calls=%fused_computation.37 | loop fusion | flops 8355840 | bytes 8519680 | tf_op jit(solution)/shard_map/reduce_sum | solution.py:33
  17.8 10.7 %fusion.23 = f32[128,256]{1,0:T(8,128)S(1)} fusion(bf16[128,256,128]{2,1,0:T(8,128)(2,1)} %param.16, f32[128,256]{1,0:T(8,128)S(1)} %broadcast_multiply_fusion), kind=kLoop, calls=%fused_computation.40 | loop fusion | flops 16744448 | bytes 8650752 | tf_op jit(solution)/shard_map/reduce_sum | solution.py:34
  28.6 11.4 %fusion.38 = f32[4,128,256]{2,0,1:T(4,128)S(1)} fusion(bf16[128,256,128]{2,1,0:T(8,128)(2,1)} %param.16, f32[128]{0:T(128)S(1)} %copy-done.5, f32[128]{0:T(128)S(1)} %copy-done.6, f32[128,256]{1,0:T(8,128)S(1)} %add_rsqrt_fusion, f32[128,256]{1,0:T(8,128)S(1)} %broadcast_multiply_fusion, bf16[128,4]{0,1:T(4,128)(2,1)S(1)} %copy-done.10), kind=kOutput, calls=%fused_computation.61 | convolution fusion | flops 58720256 | bytes 9177088 | tf_op jit(solution)/shard_map/jkc,ch->hjk/dot_general | solution.py:109
  40.1 15.1 %all-gather.3.cloned.1.call-done = bf16[16,256,128]{2,1,0:T(8,128)(2,1)} async-done(((bf16[2,256,128]{2,1,0:T(8,128)(2,1)}), bf16[16,256,128]{2,1,0:T(8,128)(2,1)}) %all-gather.3.cloned.1.call-update) | async-done | bytes 1048592 | tf_op jit(solution)/shard_map/all_gather | solution.py:101
  55.2 2.1 %dynamic-slice_select_fusion = bf16[16,128,128]{2,1,0:T(8,128)(2,1)} fusion(bf16[16,256,128]{2,1,0:T(8,128)(2,1)} %all-gather.3.cloned.1.call-done, s32[]{:T(128)S(6)} %select_n.62, pred[]{:T(512)S(6)} %eq.5), kind=kLoop, calls=%fused_computation.69 | loop fusion | flops 262144 | bytes 1048581 | tf_op jit(solution)/shard_map/jit(_where)/select_n | solution.py:8
  57.3 0.3 convert_reduce_fusion.1
  57.7 1.3 fusion.31
  59.0 1.7 convolution_convert_fusion.1
  60.7 2.5 %convolution_convert_fusion = bf16[16,256,128]{1,2,0:T(8,128)(2,1)} fusion(bf16[16,256,128]{2,1,0:T(8,128)(2,1)S(1)} %copy-done.1, f32[128]{0:T(128)S(1)} %copy-done.5, f32[128]{0:T(128)S(1)} %copy-done.6, f32[16,256]{1,0:T(8,128)S(1)} %add_rsqrt_fusion.1, f32[16,256]{1,0:T(8,128)S(1)} %broadcast_multiply_fusion.1, bf16[128,128]{1,0:T(8,128)(2,1)S(1)} %copy-done.7), kind=kOutput, calls=%fused_computation.53 | convolution fusion | flops 137887744 | bytes 2163712 | tf_op jit(solution)/shard_map/dot_general | solution.py:40
  63.2 26.5 %all-reduce.2.cloned.1.call-done = bf16[16,128,128]{2,1,0:T(8,128)(2,1)} async-done(((bf16[16,128,128]{2,1,0:T(8,128)(2,1)}), bf16[16,128,128]{2,1,0:T(8,128)(2,1)}) %all-reduce.2.cloned.1.call-update) | async-done | bytes 524304 | tf_op jit(solution)/shard_map/psum | solution.py:9
  89.7 1.2 convert_reduce_fusion.2
  91.0 1.7 fusion.41
  92.7 1.9 %fusion.35 = bf16[16,128,128]{1,2,0:T(8,128)(2,1)S(1)} fusion(bf16[16,128,128]{2,1,0:T(8,128)(2,1)} %all-reduce.2.cloned.1.call-done, f32[128]{0:T(128)S(1)} %copy-done.5, f32[128]{0:T(128)S(1)} %copy-done.6, f32[16,128]{1,0:T(8,128)S(1)} %add_rsqrt_fusion.2, f32[16,128]{1,0:T(8,128)S(1)} %broadcast_multiply_fusion.2, bf16[128,128]{1,0:T(8,128)(2,1)S(1)} %copy-done.8), kind=kOutput, calls=%fused_computation.58 | convolution fusion | flops 69206016 | bytes 1098752 | tf_op jit(solution)/shard_map/dot_general | solution.py:40
  94.6 12.7 %while.33 = (s32[]{:T(128)}, bf16[4,4,4,128]{3,2,1,0:T(4,128)(2,1)S(1)}, bf16[4,4,4,128]{3,2,1,0:T(4,128)(2,1)S(1)}, bf16[4,4,4,128,32]{3,4,2,1,0:T(8,128)(2,1)S...) while((s32[]{:T(128)}, ...), condition=%wide.region_10.11_spmd, body=%wide.region_7.10_spmd.sunk | while | flops 72871936 | bytes 8838517 | solution.py:134
  94.6 0.6 fusion.76
  95.2 0.9 fusion.77
  96.1 1.6 fusion.78
  97.8 0.6 fusion.76
  98.4 0.9 fusion.77
  99.3 1.6 fusion.78
  100.9 0.6 fusion.76
  101.5 0.9 fusion.77
  102.5 1.6 fusion.78
  104.1 0.6 fusion.76
  104.7 0.9 fusion.77
  105.6 1.6 fusion.78
  107.3 0.8 copy-done.3
  108.1 5.2 %all_gather.16 = bf16[4,16,4,128]{3,1,2,0:T(8,128)(2,1)S(1)} all-gather(bf16[1,16,4,128]{3,1,2,0:T(8,128)(2,1)S(1)} %bitcast.102), channel_id=1, replica_groups=mesh['row'=8,'col'=4] {'col'}, dimensions={0}, use_global_device_ids=true | all-gather | bytes 81920 | tf_op jit(solution)/shard_map/all_gather | solution.py:14
  113.4 5.4 %all_gather.17 = bf16[4,16,4,128]{3,1,2,0:T(8,128)(2,1)S(1)} all-gather(bf16[1,16,4,128]{3,1,2,0:T(8,128)(2,1)S(1)} %bitcast.103), channel_id=1, replica_groups=mesh['row'=8,'col'=4] {'col'}, dimensions={0}, use_global_device_ids=true | all-gather | bytes 81920 | tf_op jit(solution)/shard_map/all_gather | solution.py:14
  118.9 1.7 %fusion.49 = f32[16,128,128]{2,1,0:T(8,128)} fusion(bf16[16,128,128]{2,1,0:T(8,128)(2,1)S(1)} %copy-done.2, f32[128]{0:T(128)S(1)} %copy-done.5, f32[128]{0:T(128)S(1)} %copy-done.6, f32[16,128]{1,0:T(8,128)S(1)} %add_rsqrt_fusion.2, f32[16,128]{1,0:T(8,128)S(1)} %broadcast_multiply_fusion.2, bf16[128,128]{1,0:T(8,128)(2,1)S(1)} %copy-done.4), kind=kOutput, calls=%fused_computation.70 | convolution fusion | flops 68681728 | bytes 1623040 | tf_op jit(solution)/shard_map/dot_general | solution.py:40
  120.6 10.3 %all-gather.5.cloned.1.call-done = bf16[4,16,4,128,32]{3,4,2,1,0:T(8,128)(2,1)} async-done(((bf16[1,16,4,128,32]{3,4,2,1,0:T(8,128)(2,1)}), bf16[4,16,4,128,32]{3,4,2,1,0:T(8,128)(2,1)}) %all-gather.5.cloned.1.call-update) | async-done | bytes 2097168 | tf_op jit(solution)/shard_map/all_gather | solution.py:14
  130.9 1.2 fusion.47
  132.1 2.6 %copy.33 = f32[16,4,128,32]{3,2,1,0:T(8,128)} copy(f32[16,4,128,32]{2,3,1,0:T(8,128)S(1)} %fusion.47) | data formatting | bytes 2097152 | tf_op jit(solution)/shard_map/while | solution.py:26
  134.7 24.0 %while.34 = (s32[]{:T(128)}, f32[16,4,128]{2,1,0:T(4,128)S(1)}, f32[16,4,128]{2,1,0:T(4,128)S(1)}, f32[16,4,128,32]{3,2,1,0:T(8,128)}, bf16[4,16,4,128]{3,1,2,0:...) while((s32[]{:T(128)}, f32[16,4,128]{2,1,0:T(4,128)S(1)}, ...), condition=%wide.region_12.13_spmd, body=%wide.region_11.12_spmd.sunk | while | flops 1114117 | bytes 5079191 | solution.py:26
  134.8 1.1 constant_dynamic-slice_fusion.7
  135.9 1.0 copy.61
  136.9 5.8 %fusion.80 = f32[16,4,128,32]{3,2,1,0:T(8,128)} fusion(f32[16,4,128,32]{3,2,1,0:T(8,128)} %get-tuple-element.469, bf16[1,16,4,128,32]{4,3,2,1,0:T(8,128)(2,1)S(1)} %copy.61, f32[16,4,128]{2,1,0:T(4,128)S(1)} %get-tuple-element.424, f32[16,4,128]{2,1,0:T(4,128)S(1)} %get-tuple-element.425), kind=kLoop, calls=%fused_computation.24.clone.1 | loop fusion | flops 1048576 | bytes 2686976 | tf_op jit(solution)/shard_map/while/body/eval_jaxpr/add | solution.py:70
  142.8 1.1 constant_dynamic-slice_fusion.7
  143.9 1.0 copy.61
  145.0 5.8 %fusion.80 = f32[16,4,128,32]{3,2,1,0:T(8,128)} fusion(f32[16,4,128,32]{3,2,1,0:T(8,128)} %get-tuple-element.469, bf16[1,16,4,128,32]{4,3,2,1,0:T(8,128)(2,1)S(1)} %copy.61, f32[16,4,128]{2,1,0:T(4,128)S(1)} %get-tuple-element.424, f32[16,4,128]{2,1,0:T(4,128)S(1)} %get-tuple-element.425), kind=kLoop, calls=%fused_computation.24.clone.1 | loop fusion | flops 1048576 | bytes 2686976 | tf_op jit(solution)/shard_map/while/body/eval_jaxpr/add | solution.py:70
  150.8 1.1 constant_dynamic-slice_fusion.7
  151.9 1.0 copy.61
  153.0 5.8 %fusion.80 = f32[16,4,128,32]{3,2,1,0:T(8,128)} fusion(f32[16,4,128,32]{3,2,1,0:T(8,128)} %get-tuple-element.469, bf16[1,16,4,128,32]{4,3,2,1,0:T(8,128)(2,1)S(1)} %copy.61, f32[16,4,128]{2,1,0:T(4,128)S(1)} %get-tuple-element.424, f32[16,4,128]{2,1,0:T(4,128)S(1)} %get-tuple-element.425), kind=kLoop, calls=%fused_computation.24.clone.1 | loop fusion | flops 1048576 | bytes 2686976 | tf_op jit(solution)/shard_map/while/body/eval_jaxpr/add | solution.py:70
  158.8 2.8 %copy.37 = f32[16,4,128,32]{2,3,1,0:T(8,128)S(1)} copy(f32[16,4,128,32]{3,2,1,0:T(8,128)} %get-tuple-element.234) | data formatting | bytes 2097152 | tf_op jit(solution)/shard_map/while | solution.py:26
  161.8 1.8 %convolution_convert_fusion.2 = bf16[4,128,128]{2,1,0:T(8,128)(2,1)} fusion(f32[4,128,128]{2,1,0:T(8,128)S(1)} %copy.38, f32[16,128,128]{2,1,0:T(8,128)} %fusion.49, s32[]{:T(128)S(6)} %select_n.64, f32[128]{0:T(128)S(1)} %copy-done.12, bf16[128,128]{1,0:T(8,128)(2,1)S(1)} %copy-done.9), kind=kOutput, calls=%fused_computation.62 | convolution fusion | flops 17367040 | bytes 688644 | tf_op jit(solution)/shard_map/dot_general | solution.py:40
  (66 shorter events, 0.9 us)
Async XLA Ops:
  6.5 52.5 %copy-start = (bf16[128,128]{1,0:T(8,128)(2,1)S(1)}, bf16[128,128]{1,0:T(8,128)(2,1)}, u32[]{:S(2)}) copy-start(bf16[128,128]{1,0:T(8,128)(2,1)} %param.22) | copy-start | bytes 98308
  6.5 48.6 %all-gather.3.cloned.1.call-start = ((), (), s32[]{:S(2)}) async-start(), calls=%async_computation | async-start | bytes 1179648 | tf_op jit(solution)/shard_map/all_gather | solution.py:101
  11.9 77.8 %all-reduce.2.cloned.1.call-start = ((), (), s32[]{:S(2)}) async-start(), calls=%async_computation.1 | async-start | bytes 1048576 | tf_op jit(solution)/shard_map/psum | solution.py:9
  17.7 10.8 %copy-start.5 = (f32[128]{0:T(128)S(1)}, f32[128]{0:T(128)}, u32[]{:S(2)}) copy-start(f32[128]{0:T(128)} %param.20) | copy-start | bytes 1540
  17.7 10.8 %copy-start.6 = (f32[128]{0:T(128)S(1)}, f32[128]{0:T(128)}, u32[]{:S(2)}) copy-start(f32[128]{0:T(128)} %param.19) | copy-start | bytes 1540
  17.8 10.8 %copy-start.10 = (bf16[128,4]{0,1:T(4,128)(2,1)S(1)}, bf16[128,4]{0,1:T(4,128)(2,1)}, u32[]{:S(2)}) copy-start(bf16[128,4]{0,1:T(4,128)(2,1)} %param.26) | copy-start | bytes 3076
  28.6 11.5 %copy-start.11 = (s32[256]{0:T(256)S(1)}, s32[256]{0:T(256)}, u32[]{:S(2)}) copy-start(s32[256]{0:T(256)} %param.18) | copy-start | bytes 3076
  55.2 2.1 %copy-start.1 = (bf16[16,256,128]{2,1,0:T(8,128)(2,1)S(1)}, bf16[16,256,128]{2,1,0:T(8,128)(2,1)}, u32[]{:S(2)}) copy-start(bf16[16,256,128]{2,1,0:T(8,128)(2,1)} %all-gather.3.cloned.1.call-done) | copy-start | bytes 3145732
  57.3 73.7 %all-gather.5.cloned.1.call-start = ((), (), s32[]{:S(2)}) async-start(), calls=%async_computation.2 | async-start | bytes 2621440 | tf_op jit(solution)/shard_map/all_gather | solution.py:14
  57.7 3.0 %copy-start.7 = (bf16[128,128]{1,0:T(8,128)(2,1)S(1)}, bf16[128,128]{1,0:T(8,128)(2,1)}, u32[]{:S(2)}) copy-start(bf16[128,128]{1,0:T(8,128)(2,1)} %param.23) | copy-start | bytes 98308
  60.7 31.9 %copy-start.8 = (bf16[128,128]{1,0:T(8,128)(2,1)S(1)}, bf16[128,128]{1,0:T(8,128)(2,1)}, u32[]{:S(2)}) copy-start(bf16[128,128]{1,0:T(8,128)(2,1)} %param.21) | copy-start | bytes 98308
  94.5 24.3 %copy-start.2 = (bf16[16,128,128]{2,1,0:T(8,128)(2,1)S(1)}, bf16[16,128,128]{2,1,0:T(8,128)(2,1)}, u32[]{:S(2)}) copy-start(bf16[16,128,128]{2,1,0:T(8,128)(2,1)} %all-reduce.2.cloned.1.call-done) | copy-start | bytes 1572868
  94.6 24.3 %copy-start.4 = (bf16[128,128]{1,0:T(8,128)(2,1)S(1)}, bf16[128,128]{1,0:T(8,128)(2,1)}, u32[]{:S(2)}) copy-start(bf16[128,128]{1,0:T(8,128)(2,1)} %param.24) | copy-start | bytes 98308
  107.3 0.8 copy-start.3
  158.8 3.0 %copy-start.9 = (bf16[128,128]{1,0:T(8,128)(2,1)S(1)}, bf16[128,128]{1,0:T(8,128)(2,1)}, u32[]{:S(2)}) copy-start(bf16[128,128]{1,0:T(8,128)(2,1)} %param.27) | copy-start | bytes 98308
  158.8 3.0 %copy-start.12 = (f32[128]{0:T(128)S(1)}, f32[128]{0:T(128)}, u32[]{:S(2)}) copy-start(f32[128]{0:T(128)} %param.25) | copy-start | bytes 1540
Sparse Core Ops, SparseCore 0:
  12.1 43.0 all-gather.2
  57.5 32.1 all-reduce.1
  108.2 22.6 all-gather.4
where the time goes:
time: 171 us; the launch traced here: 170 us
  waiting for transfers between devices  52 us (30%)
  other arithmetic  46.9 us (27%)
  matrix products  29.8 us (17%)
  local copies, waits for them, and re-layouts  17 us (10%)
  between operations  13.5 us (8%)
  blocking collectives  10.7 us (6%)
    psum x1, waiting for transfers between devices, from_root(): return lax.psum(kept, axis)  26.5 us
    add x3, other arithmetic, combine_parts(): summed_a * scale_a[..., None] + summed_b * scale_b[..., None]  17.4 us
    all_gather x1, waiting for transfers between devices, body(): raw_all = lax.all_gather(raw_chosen, 'row', axis=0, tiled=True)  15.1 us
    reduce_sum x3, other arithmetic, layer_norm(): spread = jnp.mean((values - centre) ** 2, axis=-1, keepdims=True)  13.7 us
    dot_general x1, matrix products, body(): jnp.einsum('jkc,ch->hjk', normed, w_bias, preferred_element_type=jnp.floa...  11.4 us
    all_gather x2, blocking collectives, merged(): lax.all_gather(a.astype(kind), axis)  10.7 us
    all_gather x1, waiting for transfers between devices, merged(): lax.all_gather(a.astype(kind), axis)  10.3 us
    dot_general x5, matrix products, project(): jnp.dot(flat, weight, preferred_element_type=jnp.float32)  9.55 us
  transfers between devices with their start and end apart: 3, of which 3 were waited for; matrix products, arithmetic and copies ran while one was open for 21% of the time, Pallas kernels for 0%

commit v1 on v0

--- a/solution.py
+++ b/solution.py
@@ -6,7 +6,7 @@
 
 def from_root(value, axis, source):
     kept = jnp.where(lax.axis_index(axis) == source, value, 0).astype(value.dtype)
-    return lax.psum(kept, axis)
+    return jnp.sum(jax.lax.all_gather(kept, axis), 0)
 
 
 def merged(value, axis, join):

time: 171 us -> 165 us (0.965)
  waiting for transfers between devices: 52 us -> 46.5 us
    psum x1 -> x0, waiting for transfers between devices: 26.5 us -> none  [from_root(): return lax.psum(kept, axis)]
    all_gather x1, waiting for transfers between devices: 15.1 us -> 37.4 us  [body(): raw_all = lax.all_gather(raw_chosen, 'row', axis=0, tiled=True)]
    reduce_sum x0 -> x1, other arithmetic: none -> 2.03 us  [from_root(): return jnp.sum(jax.lax.all_gather(kept, axis), 0)]
  transfers between devices with their start and end apart: 3 -> 3, of which waited for: 3 -> 2; matrix products, arithmetic and copies ran while one was open for 21% -> 22% of each run, Pallas kernels for 0% -> 0%
where the time goes in v1:
time: 165 us; the launch traced here: 164 us
  other arithmetic  46.8 us (28%)
  waiting for transfers between devices  46.5 us (28%)
  matrix products  29.1 us (18%)
  local copies, waits for them, and re-layouts  17 us (10%)
  between operations  13.5 us (8%)
  blocking collectives  10.9 us (7%)
    all_gather x1, waiting for transfers between devices, body(): raw_all = lax.all_gather(raw_chosen, 'row', axis=0, tiled=True)  37.4 us
    add x3, other arithmetic, combine_parts(): summed_a * scale_a[..., None] + summed_b * scale_b[..., None]  17.4 us
    reduce_sum x3, other arithmetic, layer_norm(): spread = jnp.mean((values - centre) ** 2, axis=-1, keepdims=True)  12.6 us
    dot_general x1, matrix products, body(): jnp.einsum('jkc,ch->hjk', normed, w_bias, preferred_element_type=jnp.floa...  11.5 us
    all_gather x2, blocking collectives, merged(): lax.all_gather(a.astype(kind), axis)  10.9 us
    all_gather x1, waiting for transfers between devices, merged(): lax.all_gather(a.astype(kind), axis)  9.09 us
    dot_general x5, matrix products, project(): jnp.dot(flat, weight, preferred_element_type=jnp.float32)  8.85 us
    dot_general x4, matrix products, partial_block(): jnp.einsum('thjk,tkhd->thjd', expo.astype(jnp.bfloat16), value_block, pre...  6.4 us
  transfers between devices with their start and end apart: 3, of which 2 were waited for; matrix products, arithmetic and copies ran while one was open for 22% of the time, Pallas kernels for 0%

profile of v1, /device:TPU:0, one launch (start us, length us, event | category | flops | bytes accessed | tf_op | source)
XLA Modules:
  0.0 164.0 jit_solution(17292548208128399043)
XLA Ops:
  6.5 0.7 compare_and_fusion
  7.2 4.0 %gather_fusion = bf16[2,256,128]{2,1,0:T(8,128)(2,1)S(1)} fusion(bf16[128,256,128]{2,1,0:T(8,128)(2,1)} %param.16, s32[1024]{0:T(1024)S(1)} %pad_clamp_fusion), kind=kCustom, calls=%fused_computation | custom fusion | bytes 262152 | tf_op jit(solution)/shard_map/jit(_take)/gather | solution.py:100
  11.2 0.7 broadcast_select_fusion
  12.1 5.7 %convert_reduce_fusion = f32[128,256]{1,0:T(8,128)S(1)} fusion(bf16[128,256,128]{2,1,0:T(8,128)(2,1)} %param.16), kind=kLoop, calls=%fused_computation.37 | loop fusion | flops 8355840 | bytes 8519680 | tf_op jit(solution)/shard_map/reduce_sum | solution.py:33
  17.7 37.4 %all-gather.5.cloned.1.call-done = bf16[16,256,128]{2,1,0:T(8,128)(2,1)} async-done(((bf16[2,256,128]{2,1,0:T(8,128)(2,1)}), bf16[16,256,128]{2,1,0:T(8,128)(2,1)}) %all-gather.5.cloned.1.call-update) | async-done | bytes 1048592 | tf_op jit(solution)/shard_map/all_gather | solution.py:101
  55.1 2.0 %dynamic-slice_select_fusion = bf16[16,128,128]{2,1,0:T(8,128)(2,1)} fusion(bf16[16,256,128]{2,1,0:T(8,128)(2,1)} %all-gather.5.cloned.1.call-done, s32[]{:T(128)S(6)} %select_n.62, pred[]{:T(512)S(6)} %eq.5), kind=kLoop, calls=%fused_computation.69 | loop fusion | flops 262144 | bytes 1048581 | tf_op jit(solution)/shard_map/jit(_where)/select_n | solution.py:8
  57.2 10.7 %fusion.23 = f32[128,256]{1,0:T(8,128)S(1)} fusion(bf16[128,256,128]{2,1,0:T(8,128)(2,1)} %param.16, f32[128,256]{1,0:T(8,128)S(1)} %broadcast_multiply_fusion), kind=kLoop, calls=%fused_computation.40 | loop fusion | flops 16744448 | bytes 8650752 | tf_op jit(solution)/shard_map/reduce_sum | solution.py:34
  68.0 11.5 %fusion.38 = f32[4,128,256]{2,0,1:T(4,128)S(1)} fusion(bf16[128,256,128]{2,1,0:T(8,128)(2,1)} %param.16, f32[128]{0:T(128)S(1)} %copy-done.4, f32[128]{0:T(128)S(1)} %copy-done.5, f32[128,256]{1,0:T(8,128)S(1)} %add_rsqrt_fusion, f32[128,256]{1,0:T(8,128)S(1)} %broadcast_multiply_fusion, bf16[128,4]{0,1:T(4,128)(2,1)S(1)} %copy-done.9), kind=kOutput, calls=%fused_computation.61 | convolution fusion | flops 58720256 | bytes 9177088 | tf_op jit(solution)/shard_map/jkc,ch->hjk/dot_general | solution.py:109
  79.6 0.3 convert_reduce_fusion.1
  80.0 1.3 fusion.31
  81.3 1.7 %convolution_convert_fusion.1 = bf16[16,256,128]{1,2,0:T(8,128)(2,1)S(1)} fusion(bf16[16,256,128]{2,1,0:T(8,128)(2,1)S(1)} %copy-done.1, f32[128]{0:T(128)S(1)} %copy-done.4, f32[128]{0:T(128)S(1)} %copy-done.5, f32[16,256]{1,0:T(8,128)S(1)} %add_rsqrt_fusion.1, f32[16,256]{1,0:T(8,128)S(1)} %broadcast_multiply_fusion.1, bf16[128,128]{1,0:T(8,128)(2,1)S(1)} %copy-done), kind=kOutput, calls=%fused_computation.54 | convolution fusion | flops 137887744 | bytes 2163712 | tf_op jit(solution)/shard_map/dot_general | solution.py:40
  83.0 2.5 %convolution_convert_fusion = bf16[16,256,128]{1,2,0:T(8,128)(2,1)} fusion(bf16[16,256,128]{2,1,0:T(8,128)(2,1)S(1)} %copy-done.1, f32[128]{0:T(128)S(1)} %copy-done.4, f32[128]{0:T(128)S(1)} %copy-done.5, f32[16,256]{1,0:T(8,128)S(1)} %add_rsqrt_fusion.1, f32[16,256]{1,0:T(8,128)S(1)} %broadcast_multiply_fusion.1, bf16[128,128]{1,0:T(8,128)(2,1)S(1)} %copy-done.6), kind=kOutput, calls=%fused_computation.53 | convolution fusion | flops 137887744 | bytes 2163712 | tf_op jit(solution)/shard_map/dot_general | solution.py:40
  85.5 2.0 %reduce_sum.75 = bf16[16,128,128]{2,1,0:T(8,128)(2,1)S(1)} reduce(bf16[4,16,128,128]{3,2,1,0:T(8,128)(2,1)} %bitcast.99, bf16[]{:T(256)} %constant.148.clone.1), dimensions={0}, to_apply=%region_0.0 | reduce | flops 786432 | bytes 2621442 | tf_op jit(solution)/shard_map/reduce_sum | solution.py:9
  87.5 0.2 convert_reduce_fusion.2
  87.8 0.6 fusion.41
  88.4 1.1 fusion.35
  89.6 12.6 %while.33 = (s32[]{:T(128)}, bf16[4,4,4,128]{3,2,1,0:T(4,128)(2,1)S(1)}, bf16[4,4,4,128]{3,2,1,0:T(4,128)(2,1)S(1)}, bf16[4,4,4,128,32]{3,4,2,1,0:T(8,128)(2,1)S...) while((s32[]{:T(128)}, ...), condition=%wide.region_10.11_spmd, body=%wide.region_7.10_spmd.sunk | while | flops 72871936 | bytes 8838517 | solution.py:134
  89.6 0.6 fusion.76
  90.2 0.9 fusion.77
  91.1 1.6 fusion.78
  92.7 0.6 fusion.76
  93.3 0.9 fusion.77
  94.3 1.6 fusion.78
  95.9 0.6 fusion.76
  96.5 0.9 fusion.77
  97.4 1.6 fusion.78
  99.0 0.6 fusion.76
  99.6 0.9 fusion.77
  100.5 1.6 fusion.78
  102.2 0.8 copy-done.2
  103.0 5.2 %all_gather.24 = bf16[4,16,4,128]{3,1,2,0:T(8,128)(2,1)S(1)} all-gather(bf16[1,16,4,128]{3,1,2,0:T(8,128)(2,1)S(1)} %bitcast.104), channel_id=1, replica_groups=mesh['row'=8,'col'=4] {'col'}, dimensions={0}, use_global_device_ids=true | all-gather | bytes 81920 | tf_op jit(solution)/shard_map/all_gather | solution.py:14
  108.3 5.6 %all_gather.25 = bf16[4,16,4,128]{3,1,2,0:T(8,128)(2,1)S(1)} all-gather(bf16[1,16,4,128]{3,1,2,0:T(8,128)(2,1)S(1)} %bitcast.105), channel_id=1, replica_groups=mesh['row'=8,'col'=4] {'col'}, dimensions={0}, use_global_device_ids=true | all-gather | bytes 81920 | tf_op jit(solution)/shard_map/all_gather | solution.py:14
  113.9 1.7 %fusion.49 = f32[16,128,128]{2,1,0:T(8,128)} fusion(bf16[16,128,128]{2,1,0:T(8,128)(2,1)S(1)} %reduce_sum.75, f32[128]{0:T(128)S(1)} %copy-done.4, f32[128]{0:T(128)S(1)} %copy-done.5, f32[16,128]{1,0:T(8,128)S(1)} %add_rsqrt_fusion.2, f32[16,128]{1,0:T(8,128)S(1)} %broadcast_multiply_fusion.2, bf16[128,128]{1,0:T(8,128)(2,1)S(1)} %copy-done.3), kind=kOutput, calls=%fused_computation.70 | convolution fusion | flops 68681728 | bytes 1623040 | tf_op jit(solution)/shard_map/dot_general | solution.py:40
  115.7 9.1 %all-gather.7.cloned.1.call-done = bf16[4,16,4,128,32]{3,4,2,1,0:T(8,128)(2,1)} async-done(((bf16[1,16,4,128,32]{3,4,2,1,0:T(8,128)(2,1)}), bf16[4,16,4,128,32]{3,4,2,1,0:T(8,128)(2,1)}) %all-gather.7.cloned.1.call-update) | async-done | bytes 2097168 | tf_op jit(solution)/shard_map/all_gather | solution.py:14
  124.8 1.2 fusion.47
  125.9 2.6 %copy.33 = f32[16,4,128,32]{3,2,1,0:T(8,128)} copy(f32[16,4,128,32]{2,3,1,0:T(8,128)S(1)} %fusion.47) | data formatting | bytes 2097152 | tf_op jit(solution)/shard_map/while | solution.py:26
  128.6 24.0 %while.34 = (s32[]{:T(128)}, f32[16,4,128]{2,1,0:T(4,128)S(1)}, f32[16,4,128]{2,1,0:T(4,128)S(1)}, f32[16,4,128,32]{3,2,1,0:T(8,128)}, bf16[4,16,4,128]{3,1,2,0:...) while((s32[]{:T(128)}, f32[16,4,128]{2,1,0:T(4,128)S(1)}, ...), condition=%wide.region_12.13_spmd, body=%wide.region_11.12_spmd.sunk | while | flops 1114117 | bytes 5079191 | solution.py:26
  128.6 1.1 constant_dynamic-slice_fusion.7
  129.7 1.0 copy.61
  130.8 5.8 %fusion.80 = f32[16,4,128,32]{3,2,1,0:T(8,128)} fusion(f32[16,4,128,32]{3,2,1,0:T(8,128)} %get-tuple-element.469, bf16[1,16,4,128,32]{4,3,2,1,0:T(8,128)(2,1)S(1)} %copy.61, f32[16,4,128]{2,1,0:T(4,128)S(1)} %get-tuple-element.424, f32[16,4,128]{2,1,0:T(4,128)S(1)} %get-tuple-element.425), kind=kLoop, calls=%fused_computation.24.clone.1 | loop fusion | flops 1048576 | bytes 2686976 | tf_op jit(solution)/shard_map/while/body/eval_jaxpr/add | solution.py:70
  136.6 1.1 constant_dynamic-slice_fusion.7
  137.7 1.0 copy.61
  138.8 5.8 %fusion.80 = f32[16,4,128,32]{3,2,1,0:T(8,128)} fusion(f32[16,4,128,32]{3,2,1,0:T(8,128)} %get-tuple-element.469, bf16[1,16,4,128,32]{4,3,2,1,0:T(8,128)(2,1)S(1)} %copy.61, f32[16,4,128]{2,1,0:T(4,128)S(1)} %get-tuple-element.424, f32[16,4,128]{2,1,0:T(4,128)S(1)} %get-tuple-element.425), kind=kLoop, calls=%fused_computation.24.clone.1 | loop fusion | flops 1048576 | bytes 2686976 | tf_op jit(solution)/shard_map/while/body/eval_jaxpr/add | solution.py:70
  144.7 1.1 constant_dynamic-slice_fusion.7
  145.7 1.0 copy.61
  146.8 5.8 %fusion.80 = f32[16,4,128,32]{3,2,1,0:T(8,128)} fusion(f32[16,4,128,32]{3,2,1,0:T(8,128)} %get-tuple-element.469, bf16[1,16,4,128,32]{4,3,2,1,0:T(8,128)(2,1)S(1)} %copy.61, f32[16,4,128]{2,1,0:T(4,128)S(1)} %get-tuple-element.424, f32[16,4,128]{2,1,0:T(4,128)S(1)} %get-tuple-element.425), kind=kLoop, calls=%fused_computation.24.clone.1 | loop fusion | flops 1048576 | bytes 2686976 | tf_op jit(solution)/shard_map/while/body/eval_jaxpr/add | solution.py:70
  152.6 2.8 %copy.37 = f32[16,4,128,32]{2,3,1,0:T(8,128)S(1)} copy(f32[16,4,128,32]{3,2,1,0:T(8,128)} %get-tuple-element.234) | data formatting | bytes 2097152 | tf_op jit(solution)/shard_map/while | solution.py:26
  155.6 1.8 %convolution_convert_fusion.2 = bf16[4,128,128]{2,1,0:T(8,128)(2,1)} fusion(f32[4,128,128]{2,1,0:T(8,128)S(1)} %copy.38, f32[16,128,128]{2,1,0:T(8,128)} %fusion.49, s32[]{:T(128)S(6)} %select_n.64, f32[128]{0:T(128)S(1)} %copy-done.11, bf16[128,128]{1,0:T(8,128)(2,1)S(1)} %copy-done.8), kind=kOutput, calls=%fused_computation.62 | convolution fusion | flops 17367040 | bytes 688644 | tf_op jit(solution)/shard_map/dot_general | solution.py:40
  (65 shorter events, 0.9 us)
Async XLA Ops:
  6.5 74.8 %copy-start = (bf16[128,128]{1,0:T(8,128)(2,1)S(1)}, bf16[128,128]{1,0:T(8,128)(2,1)}, u32[]{:S(2)}) copy-start(bf16[128,128]{1,0:T(8,128)(2,1)} %param.22) | copy-start | bytes 98308
  6.5 48.6 %all-gather.5.cloned.1.call-start = ((), (), s32[]{:S(2)}) async-start(), calls=%async_computation | async-start | bytes 1179648 | tf_op jit(solution)/shard_map/all_gather | solution.py:101
  11.9 73.6 %all-gather.9.cloned.1.call-start = ((), (), s32[]{:S(2)}) async-start(), calls=%async_computation.2 | async-start | bytes 2621440 | tf_op jit(solution)/shard_map/all_gather | solution.py:9
  57.1 10.8 %copy-start.4 = (f32[128]{0:T(128)S(1)}, f32[128]{0:T(128)}, u32[]{:S(2)}) copy-start(f32[128]{0:T(128)} %param.20) | copy-start | bytes 1540
  57.1 10.8 %copy-start.5 = (f32[128]{0:T(128)S(1)}, f32[128]{0:T(128)}, u32[]{:S(2)}) copy-start(f32[128]{0:T(128)} %param.19) | copy-start | bytes 1540
  57.1 10.8 %copy-start.9 = (bf16[128,4]{0,1:T(4,128)(2,1)S(1)}, bf16[128,4]{0,1:T(4,128)(2,1)}, u32[]{:S(2)}) copy-start(bf16[128,4]{0,1:T(4,128)(2,1)} %param.26) | copy-start | bytes 3076
  57.1 67.6 %all-gather.7.cloned.1.call-start = ((), (), s32[]{:S(2)}) async-start(), calls=%async_computation.1 | async-start | bytes 2621440 | tf_op jit(solution)/shard_map/all_gather | solution.py:14
  68.0 11.6 %copy-start.10 = (s32[256]{0:T(256)S(1)}, s32[256]{0:T(256)}, u32[]{:S(2)}) copy-start(s32[256]{0:T(256)} %param.18) | copy-start | bytes 3076
  68.0 11.6 %copy-start.1 = (bf16[16,256,128]{2,1,0:T(8,128)(2,1)S(1)}, bf16[16,256,128]{2,1,0:T(8,128)(2,1)}, u32[]{:S(2)}) copy-start(bf16[16,256,128]{2,1,0:T(8,128)(2,1)} %all-gather.5.cloned.1.call-done) | copy-start | bytes 3145732
  79.9 3.1 %copy-start.6 = (bf16[128,128]{1,0:T(8,128)(2,1)S(1)}, bf16[128,128]{1,0:T(8,128)(2,1)}, u32[]{:S(2)}) copy-start(bf16[128,128]{1,0:T(8,128)(2,1)} %param.23) | copy-start | bytes 98308
  85.5 2.9 %copy-start.7 = (bf16[128,128]{1,0:T(8,128)(2,1)S(1)}, bf16[128,128]{1,0:T(8,128)(2,1)}, u32[]{:S(2)}) copy-start(bf16[128,128]{1,0:T(8,128)(2,1)} %param.21) | copy-start | bytes 98308
  89.6 24.4 %copy-start.3 = (bf16[128,128]{1,0:T(8,128)(2,1)S(1)}, bf16[128,128]{1,0:T(8,128)(2,1)}, u32[]{:S(2)}) copy-start(bf16[128,128]{1,0:T(8,128)(2,1)} %param.24) | copy-start | bytes 98308
  102.2 0.8 copy-start.2
  152.6 3.0 %copy-start.8 = (bf16[128,128]{1,0:T(8,128)(2,1)S(1)}, bf16[128,128]{1,0:T(8,128)(2,1)}, u32[]{:S(2)}) copy-start(bf16[128,128]{1,0:T(8,128)(2,1)} %param.27) | copy-start | bytes 98308
  152.6 3.0 %copy-start.11 = (f32[128]{0:T(128)S(1)}, f32[128]{0:T(128)}, u32[]{:S(2)}) copy-start(f32[128]{0:T(128)} %param.25) | copy-start | bytes 1540
Sparse Core Ops, SparseCore 0:
  12.1 42.9 all-gather.4
  57.2 21.2 all-gather.8
  103.1 21.6 all-gather.6
